TPU v7x, 32 devices: a whole 2x2x4 slice. The times are simulated.
32 devices in a mesh: outer: 1, inner: 32 (over z, y, x, core).
Axes of the slice: x: 2, y: 2, z: 4, core: 2. Of those that a mesh axis runs over, the one named last changes fastest.
Arguments:
- b_leaf: float32 [8192, 64], P(('outer', 'inner')), may hold values from -6 to 6
- b_sep: float32 [256, 64], P(('outer', 'inner')), may hold values from -6 to 6
- b_root: float32 [256, 64], P(('outer', 'inner')), may hold values from -6 to 6
- leaf_linv: float32 [8192, 256], P(('outer', 'inner')), as said below
- leaf_uinv: float32 [8192, 256], P(('outer', 'inner')), as said below
- leaf_lower: float32 [8192, 256], P(('outer', 'inner')), as said below
- leaf_upper: float32 [8192, 256], P(('outer', 'inner')), as said below
- sep_rows: int32 [32, 256], P(('outer', 'inner')), may hold values from 0 to 255, as said below
- sep_linv: float32 [256, 256], P(('outer', 'inner')), as said below
- sep_uinv: float32 [256, 256], P(('outer', 'inner')), as said below
- sep_lower: float32 [256, 256], P(None, ('outer', 'inner')), as said below
- sep_upper: float32 [256, 256], P(('outer', 'inner')), as said below
- root_linv: float32 [256, 256], P(('outer', 'inner')), as said below
- root_uinv: float32 [256, 256], P(('outer', 'inner')), as said below
- basis_leaf: float32 [8192, 512], P(('outer', 'inner')), as said below
- basis_sep: float32 [256, 512], P(('outer', 'inner')), as said below
- basis_root: float32 [256, 512], P(('outer', 'inner')), as said below
- g_blocks: float32 [32768, 128], P(('outer', 'inner')), may hold values from -0.25 to 0.25
- c_blocks: float32 [32768, 128], P(('outer', 'inner')), may hold values from -0.25 to 0.25
- block_cols: int32 [64, 4], P(('outer', 'inner')), may hold values from 0 to 1
Outputs:
- v_leaf: float32 [8192, 64], P(('outer', 'inner'))
- v_sep: float32 [256, 64], P(('outer', 'inner'))
- v_root: float32 [256, 64], P(('outer', 'inner'))
- coefficients: float32 [512, 64], replicated
- reduced_g: float32 [64, 64], replicated
- reduced_c: float32 [64, 64], replicated
Inputs may be any that keep to these rules, and one draw needn't show every extreme that they name: `sep_rows`: each row holds 256 distinct numbers; every row names 0 and 255. `leaf_linv`: lower triangular in each diagonal block of the stack, nonzero diagonal. `leaf_uinv`: upper triangular in each diagonal block of the stack, nonzero diagonal. `sep_linv`: lower triangular in each block of 256 rows, nonzero diagonal. `sep_uinv`: upper triangular in each block of 256 rows, nonzero diagonal. `root_linv`: lower triangular, nonzero diagonal. `root_uinv`: upper triangular, nonzero diagonal. `leaf_lower`: entries of order one over the square root of 256. `leaf_upper`: entries of order one over the square root of 256. `sep_lower`: entries of order one over the square root of the number of its columns. `sep_upper`: entries of order one over the square root of 256. basis_leaf, basis_sep and basis_root stacked by rows form Q with Q^T Q = 8704 I up to float32 rounding. `basis_sep`: part of the stacked Q described with basis_leaf. `basis_root`: part of the stacked Q described with basis_leaf.
All inputs are finite; a program needn't handle non-finite values.
Results may differ from a plain program's by a relative error of at most 0.0003.
Values sent between devices are 32-bit elements; how exact they have to be, the bound alone decides.
No kernel may reach another device: no remote copies, remote signals or barrier semaphores. Data moves between devices by JAX's collectives and lax.ppermute only.
A program may use at most 64 MiB of HBM per device.

v0:
```python
import jax
import jax.numpy as jnp
from jax import lax
from jax.sharding import PartitionSpec as P


def matmul_exact(left, right):
    return jnp.dot(left, right, precision=lax.Precision.HIGHEST, preferred_element_type=jnp.float32)


def contract_rows(left, right):
    return lax.dot_general(
        left,
        right,
        (((0,), (0,)), ((), ())),
        precision=lax.Precision.HIGHEST,
        preferred_element_type=jnp.float32,
    )


def shards(
    b_leaf,
    b_sep,
    b_root,
    leaf_linv,
    leaf_uinv,
    leaf_lower,
    leaf_upper,
    sep_rows,
    sep_linv,
    sep_uinv,
    sep_lower,
    sep_upper,
    root_linv,
    root_uinv,
    basis_leaf,
    basis_sep,
    basis_root,
    g_blocks,
    c_blocks,
    block_cols,
):
    ports = b_leaf.shape[1]
    sep_local = b_sep.shape[0]
    root_local = b_root.shape[0]
    sep_width = sep_linv.shape[1]
    selector = (sep_rows[0][:, None] == jnp.arange(sep_width, dtype=jnp.int32)[None, :]).astype(
        jnp.float32
    )
    y_leaf = matmul_exact(leaf_linv, b_leaf)
    contrib = matmul_exact(leaf_lower, y_leaf)
    t_sep = lax.psum_scatter(
        contract_rows(selector, contrib), "inner", scatter_dimension=0, tiled=True
    )
    sep_whole = lax.all_gather(b_sep - t_sep, "inner", axis=0, tiled=True)
    y_sep = matmul_exact(sep_linv, sep_whole)
    summed = lax.psum(matmul_exact(sep_lower, y_sep), ("outer", "inner"))
    sources = lax.all_gather(b_root, ("outer", "inner"), axis=0, tiled=True)
    y_root = matmul_exact(root_linv, sources - summed)
    y_root_all = lax.all_gather(y_root, ("outer", "inner"), axis=0, tiled=True)
    x_root = matmul_exact(root_uinv, y_root_all)
    x_root_all = lax.all_gather(x_root, ("outer", "inner"), axis=0, tiled=True)
    z_sep = y_sep - matmul_exact(sep_upper, x_root_all)
    z_sep_all = lax.all_gather(z_sep, "inner", axis=0, tiled=True)
    x_sep = matmul_exact(sep_uinv, z_sep_all)
    x_sep_all = lax.all_gather(x_sep, "inner", axis=0, tiled=True)
    coupled = matmul_exact(selector, x_sep_all)
    x_leaf = matmul_exact(leaf_uinv, y_leaf - matmul_exact(leaf_upper, coupled))
    node_count = float(
        lax.axis_size("outer") * lax.axis_size("inner") * (b_leaf.shape[0] + sep_local + root_local)
    )
    pieces_x = (x_leaf, x_sep, x_root)
    pieces_q = (basis_leaf, basis_sep, basis_root)
    projected = (
        contract_rows(basis_leaf, x_leaf)
        + contract_rows(basis_sep, x_sep)
        + contract_rows(basis_root, x_root)
    )
    coefficients = lax.psum(projected, ("outer", "inner")) / node_count
    cleaned = [
        values - matmul_exact(basis, coefficients) for basis, values in zip(pieces_q, pieces_x)
    ]
    local_gram = (
        contract_rows(cleaned[0], cleaned[0])
        + contract_rows(cleaned[1], cleaned[1])
        + contract_rows(cleaned[2], cleaned[2])
    )
    gram_matrix = lax.psum(local_gram, ("outer", "inner")) / node_count
    chol_lower = jnp.linalg.cholesky(gram_matrix)
    inverse_lower = lax.linalg.triangular_solve(
        chol_lower, jnp.eye(ports, dtype=jnp.float32), left_side=True, lower=True
    )
    v_leaf = matmul_exact(cleaned[0], inverse_lower.T)
    v_sep = matmul_exact(cleaned[1], inverse_lower.T)
    v_root = matmul_exact(cleaned[2], inverse_lower.T)
    block_rows = block_cols.shape[0]
    stored = block_cols.shape[1]
    block_size = g_blocks.shape[1]
    blocked = v_leaf.reshape(block_rows, block_size, ports)
    picked = blocked[block_cols]
    g_tiles = g_blocks.reshape(block_rows, stored, block_size, block_size)
    c_tiles = c_blocks.reshape(block_rows, stored, block_size, block_size)
    g_image = jnp.einsum("rwij,rwjp->rip", g_tiles, picked, precision=lax.Precision.HIGHEST)
    c_image = jnp.einsum("rwij,rwjp->rip", c_tiles, picked, precision=lax.Precision.HIGHEST)
    g_local = jnp.einsum("rip,riq->pq", blocked, g_image, precision=lax.Precision.HIGHEST)
    c_local = jnp.einsum("rip,riq->pq", blocked, c_image, precision=lax.Precision.HIGHEST)
    g_summed, c_summed = lax.psum((g_local, c_local), ("outer", "inner"))
    return (v_leaf, v_sep, v_root, coefficients, g_summed / node_count, c_summed / node_count)


def solution(mesh):
    return jax.shard_map(
        shards,
        mesh=mesh,
        in_specs=(
            P(("outer", "inner"), None),
            P(("outer", "inner"), None),
            P(("outer", "inner"), None),
            P(("outer", "inner"), None),
            P(("outer", "inner"), None),
            P(("outer", "inner"), None),
            P(("outer", "inner"), None),
            P(("outer", "inner"), None),
            P(("outer", "inner"), None),
            P(("outer", "inner"), None),
            P(None, ("outer", "inner")),
            P(("outer", "inner"), None),
            P(("outer", "inner"), None),
            P(("outer", "inner"), None),
            P(("outer", "inner"), None),
            P(("outer", "inner"), None),
            P(("outer", "inner"), None),
            P(("outer", "inner"), None),
            P(("outer", "inner"), None),
            P(("outer", "inner"), None),
        ),
        out_specs=(
            P(("outer", "inner"), None),
            P(("outer", "inner"), None),
            P(("outer", "inner"), None),
            P(),
            P(),
            P(),
        ),
        check_vma=False,
    )
```

profile of v0, /device:TPU:0, one launch (start us, length us, event | category | flops | bytes accessed | tf_op | source)
XLA Modules:
  0.0 685.7 jit_solution(16916968704119471954)
XLA Ops:
  7.2 1.4 fusion.17
  9.0 0.7 copy-done.16
  9.7 1.0 fusion.8
  10.8 130.4 %all-reduce.10.cloned.1.call-done = f32[256,64]{1,0:T(8,128)} async-done(((f32[256,64]{1,0:T(8,128)}), f32[256,64]{1,0:T(8,128)}) %all-reduce.10.cloned.1.call-update) | async-done | bytes 65552
  141.3 0.7 dynamic-slice_subtract_fusion
  142.0 40.0 %all_gather.18 = f32[256,64]{1,0:T(8,128)S(1)} all-gather(f32[8,64]{1,0:T(8,128)S(1)} %dynamic-slice_subtract_fusion), channel_id=1, replica_groups=mesh['outer'=1,'inner'=32] {'inner'}, dimensions={0}, use_global_device_ids=true | all-gather | bytes 67584 | tf_op jit(solution)/shard_map/all_gather | solution.py:55
  182.7 0.9 convolution_bitcast_fusion.3
  183.7 0.6 copy-done.19
  184.3 37.0 %all_gather.19 = f32[256,64]{1,0:T(8,128)S(1)} all-gather(f32[8,64]{1,0:T(8,128)S(1)} %copy-done.18), channel_id=1, replica_groups=mesh['outer'=1,'inner'=32] {'outer','inner'}, dimensions={0}, use_global_device_ids=true | all-gather | bytes 67584 | tf_op jit(solution)/shard_map/all_gather | solution.py:58
  221.4 77.8 %all-reduce.6.cloned.1.call-done = f32[256,64]{0,1:T(8,128)} async-done(((f32[256,64]{0,1:T(8,128)}), f32[256,64]{0,1:T(8,128)}) %all-reduce.6.cloned.1.call-update) | async-done | bytes 65552 | tf_op jit(solution)/shard_map/psum | solution.py:57
  299.2 1.0 convolution_bitcast_fusion.8
  300.2 40.4 %all_gather.20 = f32[256,64]{1,0:T(8,128)S(1)} all-gather(f32[8,64]{1,0:T(8,128)S(1)} %convolution_bitcast_fusion.8), channel_id=1, replica_groups=mesh['outer'=1,'inner'=32] {'outer','inner'}, dimensions={0}, use_global_device_ids=true | all-gather | bytes 67584 | tf_op jit(solution)/shard_map/all_gather | solution.py:60
  340.8 37.0 %all_gather.21 = f32[256,64]{1,0:T(8,128)S(1)} all-gather(f32[8,64]{1,0:T(8,128)S(1)} %bitcast.119), channel_id=1, replica_groups=mesh['outer'=1,'inner'=32] {'outer','inner'}, dimensions={0}, use_global_device_ids=true | all-gather | bytes 67584 | tf_op jit(solution)/shard_map/all_gather | solution.py:62
  377.9 38.3 %all_gather.22 = f32[256,64]{1,0:T(8,128)S(1)} all-gather(f32[8,64]{1,0:T(8,128)S(1)} %fusion.5), channel_id=1, replica_groups=mesh['outer'=1,'inner'=32] {'inner'}, dimensions={0}, use_global_device_ids=true | all-gather | bytes 67584 | tf_op jit(solution)/shard_map/all_gather | solution.py:64
  416.4 37.0 %all_gather.23 = f32[256,64]{1,0:T(8,128)S(1)} all-gather(f32[8,64]{1,0:T(8,128)S(1)} %bitcast.120), channel_id=1, replica_groups=mesh['outer'=1,'inner'=32] {'inner'}, dimensions={0}, use_global_device_ids=true | all-gather | bytes 67584 | tf_op jit(solution)/shard_map/all_gather | solution.py:66
  455.2 1.1 fusion.1
  456.4 122.1 %all-reduce.8.cloned.1.call-done = f32[512,64]{0,1:T(8,128)} async-done(((f32[512,64]{0,1:T(8,128)}), f32[512,64]{0,1:T(8,128)}) %all-reduce.8.cloned.1.call-update) | async-done | bytes 131088 | tf_op jit(solution)/shard_map/psum | solution.py:79
  578.5 0.9 broadcast_multiply_fusion
  579.4 0.6 convolution_subtract_fusion
  581.2 39.4 %psum.37 = f32[64,64]{0,1:T(8,128)S(1)} all-reduce(f32[64,64]{0,1:T(8,128)S(1)} %convolution_add_fusion.1), channel_id=1, replica_groups=mesh['outer'=1,'inner'=32] {'outer','inner'}, use_global_device_ids=true, to_apply=%region_3.0 | all-reduce | flops 4096 | bytes 32768 | tf_op jit(solution)/shard_map/psum | solution.py:88
  620.7 5.8 cholesky.17
  626.6 0.6 compare_reduce_fusion
  627.2 0.7 fusion.13
  627.9 4.9 custom-call.6
  633.3 0.8 fusion.27
  634.0 0.8 fusion.28
  634.8 0.6 gather_fusion
  635.4 0.7 convolution_bitcast_fusion.1
  636.4 0.7 convolution_bitcast_fusion
  637.3 40.4 %all-reduce.1 = (f32[64,64]{0,1:T(8,128)S(1)}, f32[64,64]{0,1:T(8,128)S(1)}) all-reduce(f32[64,64]{0,1:T(8,128)S(1)} %convolution_bitcast_fusion.5, f32[64,64]{0,1:T(8,128)S(1)} %convolution_bitcast_fusion.4), channel_id=1, replica_groups=mesh['outer'=1,'inner'=32] {'outer','inner'}, use_global_device_ids=true, to_apply=%region_6.7 | all-reduce | flops 8192 | bytes 65536 | tf_op jit(solution)/shard_map/psum | solution.py:107
  677.7 0.7 copy.69
  678.4 0.7 copy.70
  (73 shorter events, 6.0 us)
Async XLA Ops:
  7.2 628.2 %copy-start = (f32[1024,128]{1,0:T(8,128)S(1)}, f32[1024,128]{1,0:T(8,128)}, u32[]{:S(2)}) copy-start(f32[1024,128]{1,0:T(8,128)} %param.37) | copy-start | bytes 1572868
  7.2 1.5 copy-start.6
  7.2 134.1 %all-reduce.10.cloned.1.call-start = ((), (), s32[]{:S(2)}) async-start(), calls=%async_computation.2 | async-start | bytes 262144
  9.0 0.7 copy-start.16
  10.8 288.5 %all-reduce.6.cloned.1.call-start = ((), (), s32[]{:S(2)}) async-start(), calls=%async_computation | async-start | bytes 131072 | tf_op jit(solution)/shard_map/psum | solution.py:57
  10.8 130.5 %copy-start.17 = (f32[8,64]{1,0:T(8,128)S(1)}, f32[8,64]{1,0:T(8,128)}, u32[]{:S(2)}) copy-start(f32[8,64]{1,0:T(8,128)} %param.21) | copy-start | bytes 6148
  142.0 40.0 %copy-start.10 = (f32[8,256]{1,0:T(8,128)S(1)}, f32[8,256]{1,0:T(8,128)}, u32[]{:S(2)}) copy-start(f32[8,256]{1,0:T(8,128)} %param.28) | copy-start | bytes 24580
  182.0 0.7 copy-start.11
  183.6 0.7 copy-start.19
  183.6 0.7 copy-start.18
  183.6 394.9 %all-reduce.8.cloned.1.call-start = ((), (), s32[]{:S(2)}) async-start(), calls=%async_computation.1 | async-start | bytes 262144 | tf_op jit(solution)/shard_map/psum | solution.py:79
  221.3 78.0 %copy-start.12 = (f32[8,256]{1,0:T(8,128)S(1)}, f32[8,256]{1,0:T(8,128)}, u32[]{:S(2)}) copy-start(f32[8,256]{1,0:T(8,128)} %param.32) | copy-start | bytes 24580
  300.2 40.4 %copy-start.13 = (f32[8,256]{1,0:T(8,128)S(1)}, f32[8,256]{1,0:T(8,128)}, u32[]{:S(2)}) copy-start(f32[8,256]{1,0:T(8,128)} %param.33) | copy-start | bytes 24580
  340.8 37.0 %copy-start.14 = (f32[8,256]{1,0:T(8,128)S(1)}, f32[8,256]{1,0:T(8,128)}, u32[]{:S(2)}) copy-start(f32[8,256]{1,0:T(8,128)} %param.31) | copy-start | bytes 24580
  377.9 38.3 %copy-start.15 = (f32[8,256]{1,0:T(8,128)S(1)}, f32[8,256]{1,0:T(8,128)}, u32[]{:S(2)}) copy-start(f32[8,256]{1,0:T(8,128)} %param.29) | copy-start | bytes 24580
  416.4 37.3 %copy-start.9 = (f32[8,512]{1,0:T(8,128)S(1)}, f32[8,512]{1,0:T(8,128)}, u32[]{:S(2)}) copy-start(f32[8,512]{1,0:T(8,128)} %param.36) | copy-start | bytes 49156
  453.4 0.7 copy-start.8
  453.4 1.0 copy-start.5
  453.8 1.1 copy-start.7
  454.1 1.1 copy-start.1
  579.4 0.8 copy-start.2
  633.2 3.8 copy-start.3
  635.4 1.0 copy-start.4
Sparse Core Ops, SparseCore 0:
  14.1 127.1 all-reduce.9
  183.7 115.4 all-reduce.5
  456.5 121.9 all-reduce.7
where the time goes:
time: 686 us
  waiting for transfers between devices  330 us (48%)
  blocking collectives  309 us (45%)
  between operations  14.1 us (2%)
  other arithmetic  13.7 us (2%)
  matrix products  13.6 us (2%)
    unnamed x4, waiting for transfers between devices  130 us
    psum x1, waiting for transfers between devices, shards(): coefficients = lax.psum(projected, ('outer', 'inner')) / node_count  122 us
    psum x1, waiting for transfers between devices, shards(): summed = lax.psum(matmul_exact(sep_lower, y_sep), ('outer', 'inner'))  77.8 us
    psum x1, blocking collectives, shards(): g_summed, c_summed = lax.psum((g_local, c_local), ('outer', 'inner'))  40.4 us
    all_gather x1, blocking collectives, shards(): y_root_all = lax.all_gather(y_root, ('outer', 'inner'), axis=0, tiled=True)  40.4 us
    all_gather x1, blocking collectives, shards(): sep_whole = lax.all_gather(b_sep - t_sep, 'inner', axis=0, tiled=True)  40 us
    psum x1, blocking collectives, shards(): gram_matrix = lax.psum(local_gram, ('outer', 'inner')) / node_count  39.4 us
    all_gather x1, blocking collectives, shards(): z_sep_all = lax.all_gather(z_sep, 'inner', axis=0, tiled=True)  38.3 us
  transfers between devices with their start and end apart: 3, of which 3 were waited for; matrix products, arithmetic and copies ran while one was open for 0% of the time, Pallas kernels for 0%

commit v1 on v0

--- a/solution.py
+++ b/solution.py
@@ -2,6 +2,7 @@
 import jax.numpy as jnp
 from jax import lax
 from jax.sharding import PartitionSpec as P
+from jax.lax import psum
 
 
 def matmul_exact(left, right):
@@ -54,7 +55,8 @@
     )
     sep_whole = lax.all_gather(b_sep - t_sep, "inner", axis=0, tiled=True)
     y_sep = matmul_exact(sep_linv, sep_whole)
-    summed = lax.psum(matmul_exact(sep_lower, y_sep), ("outer", "inner"))
+    matrix = matmul_exact(sep_lower, y_sep)
+    summed = psum(psum(matrix, "outer"), axis_name="inner")
     sources = lax.all_gather(b_root, ("outer", "inner"), axis=0, tiled=True)
     y_root = matmul_exact(root_linv, sources - summed)
     y_root_all = lax.all_gather(y_root, ("outer", "inner"), axis=0, tiled=True)

time: 686 us -> 686 us (level)
  no operation moved by 1% of the time
where the time goes in v1:
time: 686 us
  waiting for transfers between devices  330 us (48%)
  blocking collectives  309 us (45%)
  between operations  14.1 us (2%)
  other arithmetic  13.7 us (2%)
  matrix products  13.6 us (2%)
    unnamed x4, waiting for transfers between devices  130 us
    psum x1, waiting for transfers between devices, shards(): coefficients = lax.psum(projected, ('outer', 'inner')) / node_count  122 us
    psum x1, waiting for transfers between devices, shards(): summed = psum(psum(matrix, 'outer'), axis_name='inner')  77.8 us
    psum x1, blocking collectives, shards(): g_summed, c_summed = lax.psum((g_local, c_local), ('outer', 'inner'))  40.4 us
    all_gather x1, blocking collectives, shards(): y_root_all = lax.all_gather(y_root, ('outer', 'inner'), axis=0, tiled=True)  40.4 us
    all_gather x1, blocking collectives, shards(): sep_whole = lax.all_gather(b_sep - t_sep, 'inner', axis=0, tiled=True)  40 us
    psum x1, blocking collectives, shards(): gram_matrix = lax.psum(local_gram, ('outer', 'inner')) / node_count  39.4 us
    all_gather x1, blocking collectives, shards(): z_sep_all = lax.all_gather(z_sep, 'inner', axis=0, tiled=True)  38.3 us
  transfers between devices with their start and end apart: 3, of which 3 were waited for; matrix products, arithmetic and copies ran while one was open for 0% of the time, Pallas kernels for 0%

profile of v1, /device:TPU:0, one launch (start us, length us, event | category | flops | bytes accessed | tf_op | source)
XLA Modules:
  0.0 685.7 jit_solution(16916968704119471954)
XLA Ops:
  7.2 1.4 fusion.17
  9.0 0.7 copy-done.16
  9.7 1.0 fusion.8
  10.8 130.4 %all-reduce.10.cloned.1.call-done = f32[256,64]{1,0:T(8,128)} async-done(((f32[256,64]{1,0:T(8,128)}), f32[256,64]{1,0:T(8,128)}) %all-reduce.10.cloned.1.call-update) | async-done | bytes 65552
  141.3 0.7 dynamic-slice_subtract_fusion
  142.0 40.0 %all_gather.18 = f32[256,64]{1,0:T(8,128)S(1)} all-gather(f32[8,64]{1,0:T(8,128)S(1)} %dynamic-slice_subtract_fusion), channel_id=1, replica_groups=mesh['outer'=1,'inner'=32] {'inner'}, dimensions={0}, use_global_device_ids=true | all-gather | bytes 67584 | tf_op jit(solution)/shard_map/all_gather | solution.py:56
  182.7 0.9 convolution_bitcast_fusion.3
  183.7 0.6 copy-done.19
  184.3 37.0 %all_gather.19 = f32[256,64]{1,0:T(8,128)S(1)} all-gather(f32[8,64]{1,0:T(8,128)S(1)} %copy-done.18), channel_id=1, replica_groups=mesh['outer'=1,'inner'=32] {'outer','inner'}, dimensions={0}, use_global_device_ids=true | all-gather | bytes 67584 | tf_op jit(solution)/shard_map/all_gather | solution.py:60
  221.4 77.8 %all-reduce.6.cloned.1.call-done = f32[256,64]{0,1:T(8,128)} async-done(((f32[256,64]{0,1:T(8,128)}), f32[256,64]{0,1:T(8,128)}) %all-reduce.6.cloned.1.call-update) | async-done | bytes 65552 | tf_op jit(solution)/shard_map/psum | solution.py:59
  299.2 1.0 convolution_bitcast_fusion.8
  300.2 40.4 %all_gather.20 = f32[256,64]{1,0:T(8,128)S(1)} all-gather(f32[8,64]{1,0:T(8,128)S(1)} %convolution_bitcast_fusion.8), channel_id=1, replica_groups=mesh['outer'=1,'inner'=32] {'outer','inner'}, dimensions={0}, use_global_device_ids=true | all-gather | bytes 67584 | tf_op jit(solution)/shard_map/all_gather | solution.py:62
  340.8 37.0 %all_gather.21 = f32[256,64]{1,0:T(8,128)S(1)} all-gather(f32[8,64]{1,0:T(8,128)S(1)} %bitcast.119), channel_id=1, replica_groups=mesh['outer'=1,'inner'=32] {'outer','inner'}, dimensions={0}, use_global_device_ids=true | all-gather | bytes 67584 | tf_op jit(solution)/shard_map/all_gather | solution.py:64
  377.9 38.3 %all_gather.22 = f32[256,64]{1,0:T(8,128)S(1)} all-gather(f32[8,64]{1,0:T(8,128)S(1)} %fusion.5), channel_id=1, replica_groups=mesh['outer'=1,'inner'=32] {'inner'}, dimensions={0}, use_global_device_ids=true | all-gather | bytes 67584 | tf_op jit(solution)/shard_map/all_gather | solution.py:66
  416.4 37.0 %all_gather.23 = f32[256,64]{1,0:T(8,128)S(1)} all-gather(f32[8,64]{1,0:T(8,128)S(1)} %bitcast.120), channel_id=1, replica_groups=mesh['outer'=1,'inner'=32] {'inner'}, dimensions={0}, use_global_device_ids=true | all-gather | bytes 67584 | tf_op jit(solution)/shard_map/all_gather | solution.py:68
  455.2 1.1 fusion.1
  456.4 122.1 %all-reduce.8.cloned.1.call-done = f32[512,64]{0,1:T(8,128)} async-done(((f32[512,64]{0,1:T(8,128)}), f32[512,64]{0,1:T(8,128)}) %all-reduce.8.cloned.1.call-update) | async-done | bytes 131088 | tf_op jit(solution)/shard_map/psum | solution.py:81
  578.5 0.9 broadcast_multiply_fusion
  579.4 0.6 convolution_subtract_fusion
  581.2 39.4 %psum.40 = f32[64,64]{0,1:T(8,128)S(1)} all-reduce(f32[64,64]{0,1:T(8,128)S(1)} %convolution_add_fusion.1), channel_id=1, replica_groups=mesh['outer'=1,'inner'=32] {'outer','inner'}, use_global_device_ids=true, to_apply=%region_3.0 | all-reduce | flops 4096 | bytes 32768 | tf_op jit(solution)/shard_map/psum | solution.py:90
  620.7 5.8 cholesky.17
  626.6 0.6 compare_reduce_fusion
  627.2 0.7 fusion.13
  627.9 4.9 custom-call.6
  633.3 0.8 fusion.27
  634.0 0.8 fusion.28
  634.8 0.6 gather_fusion
  635.4 0.7 convolution_bitcast_fusion.1
  636.4 0.7 convolution_bitcast_fusion
  637.3 40.4 %all-reduce.1 = (f32[64,64]{0,1:T(8,128)S(1)}, f32[64,64]{0,1:T(8,128)S(1)}) all-reduce(f32[64,64]{0,1:T(8,128)S(1)} %convolution_bitcast_fusion.5, f32[64,64]{0,1:T(8,128)S(1)} %convolution_bitcast_fusion.4), channel_id=1, replica_groups=mesh['outer'=1,'inner'=32] {'outer','inner'}, use_global_device_ids=true, to_apply=%region_6.7 | all-reduce | flops 8192 | bytes 65536 | tf_op jit(solution)/shard_map/psum | solution.py:109
  677.7 0.7 copy.69
  678.4 0.7 copy.70
  (73 shorter events, 6.0 us)
Async XLA Ops:
  7.2 628.2 %copy-start = (f32[1024,128]{1,0:T(8,128)S(1)}, f32[1024,128]{1,0:T(8,128)}, u32[]{:S(2)}) copy-start(f32[1024,128]{1,0:T(8,128)} %param.37) | copy-start | bytes 1572868
  7.2 1.5 copy-start.6
  7.2 134.1 %all-reduce.10.cloned.1.call-start = ((), (), s32[]{:S(2)}) async-start(), calls=%async_computation.2 | async-start | bytes 262144
  9.0 0.7 copy-start.16
  10.8 288.5 %all-reduce.6.cloned.1.call-start = ((), (), s32[]{:S(2)}) async-start(), calls=%async_computation | async-start | bytes 131072 | tf_op jit(solution)/shard_map/psum | solution.py:59
  10.8 130.5 %copy-start.17 = (f32[8,64]{1,0:T(8,128)S(1)}, f32[8,64]{1,0:T(8,128)}, u32[]{:S(2)}) copy-start(f32[8,64]{1,0:T(8,128)} %param.21) | copy-start | bytes 6148
  142.0 40.0 %copy-start.10 = (f32[8,256]{1,0:T(8,128)S(1)}, f32[8,256]{1,0:T(8,128)}, u32[]{:S(2)}) copy-start(f32[8,256]{1,0:T(8,128)} %param.28) | copy-start | bytes 24580
  182.0 0.7 copy-start.11
  183.6 0.7 copy-start.19
  183.6 0.7 copy-start.18
  183.6 394.9 %all-reduce.8.cloned.1.call-start = ((), (), s32[]{:S(2)}) async-start(), calls=%async_computation.1 | async-start | bytes 262144 | tf_op jit(solution)/shard_map/psum | solution.py:81
  221.3 78.0 %copy-start.12 = (f32[8,256]{1,0:T(8,128)S(1)}, f32[8,256]{1,0:T(8,128)}, u32[]{:S(2)}) copy-start(f32[8,256]{1,0:T(8,128)} %param.32) | copy-start | bytes 24580
  300.2 40.4 %copy-start.13 = (f32[8,256]{1,0:T(8,128)S(1)}, f32[8,256]{1,0:T(8,128)}, u32[]{:S(2)}) copy-start(f32[8,256]{1,0:T(8,128)} %param.33) | copy-start | bytes 24580
  340.8 37.0 %copy-start.14 = (f32[8,256]{1,0:T(8,128)S(1)}, f32[8,256]{1,0:T(8,128)}, u32[]{:S(2)}) copy-start(f32[8,256]{1,0:T(8,128)} %param.31) | copy-start | bytes 24580
  377.9 38.3 %copy-start.15 = (f32[8,256]{1,0:T(8,128)S(1)}, f32[8,256]{1,0:T(8,128)}, u32[]{:S(2)}) copy-start(f32[8,256]{1,0:T(8,128)} %param.29) | copy-start | bytes 24580
  416.4 37.3 %copy-start.9 = (f32[8,512]{1,0:T(8,128)S(1)}, f32[8,512]{1,0:T(8,128)}, u32[]{:S(2)}) copy-start(f32[8,512]{1,0:T(8,128)} %param.36) | copy-start | bytes 49156
  453.4 0.7 copy-start.8
  453.4 1.0 copy-start.5
  453.8 1.1 copy-start.7
  454.1 1.1 copy-start.1
  579.4 0.8 copy-start.2
  633.2 3.8 copy-start.3
  635.4 1.0 copy-start.4
Sparse Core Ops, SparseCore 0:
  14.1 127.1 all-reduce.9
  183.7 115.4 all-reduce.5
  456.5 121.9 all-reduce.7
